TPU v7x, 32 devices: a whole 2x2x4 slice. The times are simulated.
32 devices in a mesh: tm: 8 (over z, y), space: 4 (over x, core).
Axes of the slice: x: 2, y: 2, z: 4, core: 2. Of those that a mesh axis runs over, the one named last changes fastest.
Arguments:
- initial_guess: float32 [8, 1024, 1024], P('tm', 'space'), may hold values from -6 to 6
- start_field: float32 [1024, 1024], P('space'), may hold values from -6 to 6
- source_field: float32 [1024, 1024], P('space'), may hold values from -0.3 to 0.3
Outputs:
- final_states: float32 [8, 1024, 1024], P('tm', 'space')
All inputs are finite; a program needn't handle non-finite values.
Results may differ from a plain program's by a relative error of at most 0.00013.
Values sent between devices are 32-bit elements; how exact they have to be, the bound alone decides.
A program may use at most 64 MiB of HBM per device.

v0:
```python
import jax
import jax.numpy as jnp
from jax import lax
from jax.sharding import PartitionSpec as P

M = 16


decay_rate = 0.0005
spread_rate = 0.01


def shifted(value, axis, steps):
    count = lax.axis_size(axis)
    first, last = (max(0, -steps), min(count, count - steps))
    return lax.ppermute(value, axis, [(source, source + steps) for source in range(first, last)])


def cas_matrix(length):
    indices = jnp.arange(length, dtype=jnp.int32)
    product = indices[:, None] * indices[None, :] % length
    angles = 2.0 * jnp.pi / length * product.astype(jnp.float32)
    return jnp.cos(angles) + jnp.sin(angles)


def local_symbols(length, column_width):
    offset = lax.axis_index("space") * column_width
    row_modes = jnp.arange(length, dtype=jnp.int32).astype(jnp.float32)
    column_modes = (offset + jnp.arange(column_width, dtype=jnp.int32)).astype(jnp.float32)
    row_sines = jnp.sin(jnp.pi * row_modes / length) ** 2
    column_sines = jnp.sin(jnp.pi * column_modes / length) ** 2
    stiffness = 4.0 * (row_sines[:, None] + column_sines[None, :])
    fine_factor = 1.0 / (1.0 + decay_rate + spread_rate * stiffness)
    coarse_factor = 1.0 / (1.0 + M * decay_rate + M * spread_rate * stiffness)
    fine_power = jnp.ones_like(fine_factor)
    forcing_symbol = jnp.zeros_like(fine_factor)
    for substep in range(M):
        fine_power = fine_power * fine_factor
        forcing_symbol = forcing_symbol + fine_power
    return (fine_power, forcing_symbol, coarse_factor)


def forward(fields, kernel):
    along_rows = jnp.einsum("brj,jk->brk", fields, kernel, precision=lax.Precision.HIGHEST)
    columns = lax.all_to_all(along_rows, "space", split_axis=2, concat_axis=1, tiled=True)
    return jnp.einsum("ij,bjk->bik", kernel, columns, precision=lax.Precision.HIGHEST)


def inverse(spectra, kernel):
    length = kernel.shape[0]
    along_columns = jnp.einsum("ij,bjk->bik", kernel, spectra, precision=lax.Precision.HIGHEST)
    row_layout = lax.all_to_all(along_columns, "space", split_axis=1, concat_axis=2, tiled=True)
    restored = jnp.einsum("brj,jk->brk", row_layout, kernel, precision=lax.Precision.HIGHEST)
    return restored / float(length * length)


def previous(states, start_state, at_start):
    incoming = shifted(states[-1], "tm", 1)
    first_state = jnp.where(at_start, start_state, incoming)
    return jnp.concatenate([first_state[None], states[:-1]], axis=0)


def coarse_chain(residual_hat, coarse_factor):
    blocks = residual_hat.shape[0]
    running = jnp.zeros_like(residual_hat[0])
    position = 0
    running = coarse_factor * running + residual_hat[position]
    partial_value = [running]
    block_factor = coarse_factor**blocks
    relay_turns = lax.axis_size("tm") - 1

    def relay_turn(turn_index, carried):
        outgoing = block_factor * carried + running
        return shifted(outgoing, "tm", 1)

    entering = lax.fori_loop(0, relay_turns, relay_turn, jnp.zeros_like(running))
    lifting = jnp.ones_like(coarse_factor)
    position = 0
    lifting = lifting * coarse_factor
    errors = [partial_value[position] + lifting * entering]
    return jnp.stack(errors, axis=0)


def body(initial_guess, start_field, source_field):
    length = start_field.shape[1]
    column_width = length // lax.axis_size("space")
    kernel = cas_matrix(length)
    fine_power, forcing_symbol, coarse_factor = local_symbols(length, column_width)
    at_start = lax.axis_index("tm") == 0
    blocks = initial_guess.shape[0]
    stacked = jnp.concatenate([initial_guess, start_field[None], source_field[None]], axis=0)
    spectra = forward(stacked, kernel)
    states = spectra[:blocks]
    start_state = spectra[blocks]
    forcing = forcing_symbol * spectra[blocks + 1]
    relaxed = fine_power * previous(states, start_state, at_start) + forcing
    residual = fine_power * previous(relaxed, start_state, at_start) + forcing - relaxed
    states = relaxed + coarse_chain(residual, coarse_factor)
    return inverse(states, kernel)


def solution(mesh):
    return jax.shard_map(
        body,
        mesh=mesh,
        in_specs=(P("tm", "space", None), P("space", None), P("space", None)),
        out_specs=P("tm", "space", None),
        check_vma=False,
    )
```

profile of v0, /device:TPU:16, one launch (start us, length us, event | category | flops | bytes accessed | tf_op | source)
XLA Modules:
  0.0 402.9 jit_solution(6113995466226512795)
XLA Ops:
  0.0 2.1 fusion.99
  2.1 28.3 %fusion.8 = f32[3,256,1024]{2,1,0:T(8,128)S(1)} fusion(f32[3,256,1024]{2,1,0:T(8,128)S(1)} %fusion.99), kind=kOutput, calls=%fused_computation.11 | convolution fusion | flops 9679405056 | bytes 6291456 | tf_op jit(solution)/shard_map/brj,jk->brk/dot_general | solution.py:44
  30.4 3.3 copy.19
  33.6 5.0 %all-to-all-start = ((f32[3,256,1024]{1,0,2:T(4,128)}), f32[3,256,1024]{1,0,2:T(4,128)}, u32[]{:S(2)}, u32[]{:S(2)}) async-start(f32[3,256,1024]{1,0,2:T(4,128)} %copy.19), calls=%async_computation | async-start | bytes 8388608 | tf_op jit(solution)/shard_map/all_to_all | solution.py:45
  38.6 17.5 %fusion.101 = f32[1024,1024,1]{1,0,2:T(8,128)} fusion(), kind=kLoop, calls=%fused_computation.10.clone.clone.clone.1 | loop fusion | flops 15728640 | bytes 4194304 | tf_op jit(solution)/shard_map/ij,bjk->bik/dot_general | solution.py:46
  56.2 30.7 %all-to-all-done = f32[3,256,1024]{1,0,2:T(4,128)} async-done(((f32[3,256,1024]{1,0,2:T(4,128)}), f32[3,256,1024]{1,0,2:T(4,128)}, u32[]{:S(2)}, u32[]{:S(2)}) %all-to-all-start) | async-done | bytes 3145760 | tf_op jit(solution)/shard_map/all_to_all | solution.py:45
  86.8 4.2 %copy.28 = f32[3,256,4,256]{1,2,3,0:T(4,128)S(1)} copy(f32[3,256,4,256]{1,0,3,2:T(4,128)} %bitcast.3) | data formatting | bytes 6291456 | tf_op jit(solution)/shard_map/all_to_all | solution.py:45
  91.0 3.1 all_to_all.27
  94.1 13.3 %fusion.20 = f32[3,1024,256]{1,2,0:T(8,128)S(1)} fusion(f32[3,1024,256]{1,2,0:T(8,128)} %all_to_all.27, f32[1024,1024,1]{1,0,2:T(8,128)} %fusion.101), kind=kOutput, calls=%fused_computation.27 | convolution fusion | flops 9663676416 | bytes 10485760 | tf_op jit(solution)/shard_map/ij,bjk->bik/dot_general | solution.py:46
  107.4 1.0 slice_bitcast_fusion.1
  108.4 3.4 collective-permute-start.1
  111.9 24.2 %collective-permute-done.1 = f32[1024,256]{0,1:T(8,128)} collective-permute-done((f32[1024,256]{0,1:T(8,128)}, f32[1024,256]{0,1:T(8,128)}, u32[]{:S(2)}, u32[]{:S(2)}) %collective-permute-start.1) | collective-permute-done | bytes 1048608 | tf_op jit(solution)/shard_map/ppermute | solution.py:16
  136.1 2.6 multiply_add_fusion.1
  138.7 0.0 copy-start
  138.7 2.5 collective-permute-start.2
  141.2 24.0 %collective-permute-done.2 = f32[1024,256]{0,1:T(8,128)S(1)} collective-permute-done((f32[1024,256]{0,1:T(8,128)S(1)}, f32[1024,256]{0,1:T(8,128)S(1)}, u32[]{:S(2)}, u32[]{:S(2)}) %collective-permute-start.2) | collective-permute-done | bytes 1048608 | tf_op jit(solution)/shard_map/ppermute | solution.py:16
  165.2 0.0 copy-done
  165.2 2.0 subtract_add_fusion
  167.2 1.6 copy.22
  168.8 0.1 broadcast.36.clone
  168.9 166.4 %while.11 = (s32[]{:T(128)}, f32[1024,256]{1,0:T(8,128)S(1)}, f32[1024,256]{1,0:T(8,128)S(1)}, f32[256]{0:T(256)S(1)}, f32[1024]{0:T(1024)S(1)}, /*index=5*/s32[]{:T(128)}) while((s32[]{:T(128)}, f32[1024,256]{1,0:T(8,128)S(1)}, f32[1024,256]{1,0:T(8,128)S(1)}, f32[256]{0:T(256)S(1)}, f32[1024]{0:T(1024)S(1)}, ...), condition=%wide.region_1.2_spmd.clone, body=%wide.region_0.1_spmd.clone.sunk | while | flops 1572866 | bytes 7345261 | solution.py:76
  169.1 0.3 fusion.104
  169.4 1.9 collective-permute-start
  171.3 23.7 %collective-permute-done = f32[1024,256]{1,0:T(8,128)S(1)} collective-permute-done((f32[1024,256]{1,0:T(8,128)S(1)}, f32[1024,256]{1,0:T(8,128)S(1)}, u32[]{:S(2)}, u32[]{:S(2)}) %collective-permute-start) | collective-permute-done | bytes 1048608 | tf_op jit(solution)/shard_map/while/body/eval_jaxpr/ppermute | solution.py:16
  195.1 0.3 fusion.104
  195.3 1.9 collective-permute-start
  197.3 22.9 %collective-permute-done = f32[1024,256]{1,0:T(8,128)S(1)} collective-permute-done((f32[1024,256]{1,0:T(8,128)S(1)}, f32[1024,256]{1,0:T(8,128)S(1)}, u32[]{:S(2)}, u32[]{:S(2)}) %collective-permute-start) | collective-permute-done | bytes 1048608 | tf_op jit(solution)/shard_map/while/body/eval_jaxpr/ppermute | solution.py:16
  220.2 0.3 fusion.104
  220.4 1.9 collective-permute-start
  222.4 22.0 %collective-permute-done = f32[1024,256]{1,0:T(8,128)S(1)} collective-permute-done((f32[1024,256]{1,0:T(8,128)S(1)}, f32[1024,256]{1,0:T(8,128)S(1)}, u32[]{:S(2)}, u32[]{:S(2)}) %collective-permute-start) | collective-permute-done | bytes 1048608 | tf_op jit(solution)/shard_map/while/body/eval_jaxpr/ppermute | solution.py:16
  244.4 0.3 fusion.104
  244.7 1.9 collective-permute-start
  246.6 21.2 %collective-permute-done = f32[1024,256]{1,0:T(8,128)S(1)} collective-permute-done((f32[1024,256]{1,0:T(8,128)S(1)}, f32[1024,256]{1,0:T(8,128)S(1)}, u32[]{:S(2)}, u32[]{:S(2)}) %collective-permute-start) | collective-permute-done | bytes 1048608 | tf_op jit(solution)/shard_map/while/body/eval_jaxpr/ppermute | solution.py:16
  267.8 0.3 fusion.104
  268.1 1.9 collective-permute-start
  270.0 21.1 %collective-permute-done = f32[1024,256]{1,0:T(8,128)S(1)} collective-permute-done((f32[1024,256]{1,0:T(8,128)S(1)}, f32[1024,256]{1,0:T(8,128)S(1)}, u32[]{:S(2)}, u32[]{:S(2)}) %collective-permute-start) | collective-permute-done | bytes 1048608 | tf_op jit(solution)/shard_map/while/body/eval_jaxpr/ppermute | solution.py:16
  291.1 0.3 fusion.104
  291.4 1.9 collective-permute-start
  293.3 21.1 %collective-permute-done = f32[1024,256]{1,0:T(8,128)S(1)} collective-permute-done((f32[1024,256]{1,0:T(8,128)S(1)}, f32[1024,256]{1,0:T(8,128)S(1)}, u32[]{:S(2)}, u32[]{:S(2)}) %collective-permute-start) | collective-permute-done | bytes 1048608 | tf_op jit(solution)/shard_map/while/body/eval_jaxpr/ppermute | solution.py:16
  314.4 0.3 fusion.104
  314.7 1.9 collective-permute-start
  316.7 18.6 %collective-permute-done = f32[1024,256]{1,0:T(8,128)S(1)} collective-permute-done((f32[1024,256]{1,0:T(8,128)S(1)}, f32[1024,256]{1,0:T(8,128)S(1)}, u32[]{:S(2)}, u32[]{:S(2)}) %collective-permute-start) | collective-permute-done | bytes 1048608 | tf_op jit(solution)/shard_map/while/body/eval_jaxpr/ppermute | solution.py:16
  335.3 0.3 copy.23
  335.6 22.8 %fusion.27 = f32[1,1024,256]{1,2,0:T(8,128)S(1)} fusion(f32[1024,256]{0,1:T(8,128)} %copy-done, f32[1024,256]{0,1:T(8,128)} %subtract_add_fusion, f32[1024,256]{0,1:T(8,128)S(1)} %copy.23, f32[256]{0:T(256)S(1)} %get-tuple-element.130, f32[1024]{0:T(1024)S(1)} %get-tuple-element.129), kind=kOutput, calls=%fused_computation.34 | convolution fusion | flops 3238789120 | bytes 4199424 | tf_op jit(solution)/shard_map/ij,bjk->bik/dot_general | solution.py:51
  358.4 0.8 copy.24
  359.2 18.7 %all_to_all.33 = f32[1,1024,256]{2,0,1:T(1,128)S(1)} all-to-all(f32[1,1024,256]{2,0,1:T(1,128)S(1)} %copy.24), channel_id=1, replica_groups=mesh['tm'=8,'space'=4] {'space'}, dimensions={1} | all-to-all | bytes 2097152 | tf_op jit(solution)/shard_map/all_to_all | solution.py:52
  377.9 0.1 copy.26
  377.9 0.3 copy.25
  378.3 24.2 %fusion.29 = f32[1,256,1024]{2,1,0:T(8,128)} fusion(f32[256,1024]{0,1:T(8,128)S(1)} %bitcast.54), kind=kOutput, calls=%fused_computation.36 | convolution fusion | flops 3237216256 | bytes 2097152 | tf_op jit(solution)/shard_map/brj,jk->brk/dot_general | solution.py:53
  (2 shorter events, 0.1 us)
Async XLA Ops:
  33.6 53.2 %all-to-all-start = ((f32[3,256,1024]{1,0,2:T(4,128)}), f32[3,256,1024]{1,0,2:T(4,128)}, u32[]{:S(2)}, u32[]{:S(2)}) async-start(f32[3,256,1024]{1,0,2:T(4,128)} %copy.19), calls=%async_computation | async-start | bytes 8388608 | tf_op jit(solution)/shard_map/all_to_all | solution.py:45
  108.4 27.7 %collective-permute-start.1 = (f32[1024,256]{0,1:T(8,128)}, f32[1024,256]{0,1:T(8,128)}, u32[]{:S(2)}, u32[]{:S(2)}) collective-permute-start(f32[1024,256]{0,1:T(8,128)} %slice_bitcast_fusion.1), channel_id=1, source_target_pairs={{0,4},{4,8},{8,12},{12,16},{16,20},{20,24},{24,28},{1,5},{5,9},{9,... | collective-permute-start | bytes 3145736 | tf_op jit(solution)/shard_map/ppermute | solution.py:16
  138.7 26.5 %copy-start = (f32[1024,256]{0,1:T(8,128)}, f32[1024,256]{0,1:T(8,128)S(1)}, u32[]{:S(2)}) copy-start(f32[1024,256]{0,1:T(8,128)S(1)} %get-tuple-element.72) | copy-start | bytes 3145732
  138.7 26.5 %collective-permute-start.2 = (f32[1024,256]{0,1:T(8,128)S(1)}, f32[1024,256]{0,1:T(8,128)S(1)}, u32[]{:S(2)}, u32[]{:S(2)}) collective-permute-start(f32[1024,256]{0,1:T(8,128)S(1)} %get-tuple-element.72), channel_id=1, source_target_pairs={{0,4},{4,8},{8,12},{12,16},{16,20},{20,24},{24,28},{1,5},{5,9},{9,... | collective-permute-start | bytes 3145736 | tf_op jit(solution)/shard_map/ppermute | solution.py:16
  169.4 25.7 %collective-permute-start = (f32[1024,256]{1,0:T(8,128)S(1)}, f32[1024,256]{1,0:T(8,128)S(1)}, u32[]{:S(2)}, u32[]{:S(2)}) collective-permute-start(f32[1024,256]{1,0:T(8,128)S(1)} %fusion.104), channel_id=1, source_target_pairs={{0,4},{4,8},{8,12},{12,16},{16,20},{20,24},{24,28},{1,5},{5,9},{9,... | collective-permute-start | bytes 3145736 | tf_op jit(solution)/shard_map/while/body/eval_jaxpr/ppermute | solution.py:16
  195.3 24.8 %collective-permute-start = (f32[1024,256]{1,0:T(8,128)S(1)}, f32[1024,256]{1,0:T(8,128)S(1)}, u32[]{:S(2)}, u32[]{:S(2)}) collective-permute-start(f32[1024,256]{1,0:T(8,128)S(1)} %fusion.104), channel_id=1, source_target_pairs={{0,4},{4,8},{8,12},{12,16},{16,20},{20,24},{24,28},{1,5},{5,9},{9,... | collective-permute-start | bytes 3145736 | tf_op jit(solution)/shard_map/while/body/eval_jaxpr/ppermute | solution.py:16
  220.4 24.0 %collective-permute-start = (f32[1024,256]{1,0:T(8,128)S(1)}, f32[1024,256]{1,0:T(8,128)S(1)}, u32[]{:S(2)}, u32[]{:S(2)}) collective-permute-start(f32[1024,256]{1,0:T(8,128)S(1)} %fusion.104), channel_id=1, source_target_pairs={{0,4},{4,8},{8,12},{12,16},{16,20},{20,24},{24,28},{1,5},{5,9},{9,... | collective-permute-start | bytes 3145736 | tf_op jit(solution)/shard_map/while/body/eval_jaxpr/ppermute | solution.py:16
  244.7 23.1 %collective-permute-start = (f32[1024,256]{1,0:T(8,128)S(1)}, f32[1024,256]{1,0:T(8,128)S(1)}, u32[]{:S(2)}, u32[]{:S(2)}) collective-permute-start(f32[1024,256]{1,0:T(8,128)S(1)} %fusion.104), channel_id=1, source_target_pairs={{0,4},{4,8},{8,12},{12,16},{16,20},{20,24},{24,28},{1,5},{5,9},{9,... | collective-permute-start | bytes 3145736 | tf_op jit(solution)/shard_map/while/body/eval_jaxpr/ppermute | solution.py:16
  268.1 23.0 %collective-permute-start = (f32[1024,256]{1,0:T(8,128)S(1)}, f32[1024,256]{1,0:T(8,128)S(1)}, u32[]{:S(2)}, u32[]{:S(2)}) collective-permute-start(f32[1024,256]{1,0:T(8,128)S(1)} %fusion.104), channel_id=1, source_target_pairs={{0,4},{4,8},{8,12},{12,16},{16,20},{20,24},{24,28},{1,5},{5,9},{9,... | collective-permute-start | bytes 3145736 | tf_op jit(solution)/shard_map/while/body/eval_jaxpr/ppermute | solution.py:16
  291.4 23.0 %collective-permute-start = (f32[1024,256]{1,0:T(8,128)S(1)}, f32[1024,256]{1,0:T(8,128)S(1)}, u32[]{:S(2)}, u32[]{:S(2)}) collective-permute-start(f32[1024,256]{1,0:T(8,128)S(1)} %fusion.104), channel_id=1, source_target_pairs={{0,4},{4,8},{8,12},{12,16},{16,20},{20,24},{24,28},{1,5},{5,9},{9,... | collective-permute-start | bytes 3145736 | tf_op jit(solution)/shard_map/while/body/eval_jaxpr/ppermute | solution.py:16
  314.7 20.5 %collective-permute-start = (f32[1024,256]{1,0:T(8,128)S(1)}, f32[1024,256]{1,0:T(8,128)S(1)}, u32[]{:S(2)}, u32[]{:S(2)}) collective-permute-start(f32[1024,256]{1,0:T(8,128)S(1)} %fusion.104), channel_id=1, source_target_pairs={{0,4},{4,8},{8,12},{12,16},{16,20},{20,24},{24,28},{1,5},{5,9},{9,... | collective-permute-start | bytes 3145736 | tf_op jit(solution)/shard_map/while/body/eval_jaxpr/ppermute | solution.py:16
where the time goes:
time: 409 us; the launch traced here: 403 us
  waiting for transfers between devices  229 us (56%)
  matrix products  88.5 us (22%)
  other arithmetic  26.2 us (6%)
  starting transfers between devices  24.4 us (6%)
  blocking collectives  18.7 us (5%)
  local copies, waits for them, and re-layouts  14.7 us (4%)
    ppermute x9, waiting for transfers between devices, shifted(): lax.ppermute(value, axis, [(source, source + steps) for source in range(f...  199 us
    all_to_all x1, waiting for transfers between devices, forward(): lax.all_to_all(along_rows, 'space', split_axis=2, concat_axis=1, tiled=True)  30.7 us
    dot_general x1, matrix products, forward(): jnp.einsum('brj,jk->brk', fields, kernel, precision=lax.Precision.HIGHEST)  28.3 us
    dot_general x1, matrix products, inverse(): jnp.einsum('brj,jk->brk', row_layout, kernel, precision=lax.Precision.HIG...  24.2 us
    dot_general x1, matrix products, inverse(): jnp.einsum('ij,bjk->bik', kernel, spectra, precision=lax.Precision.HIGHEST)  22.8 us
    ppermute x9, starting transfers between devices, shifted(): lax.ppermute(value, axis, [(source, source + steps) for source in range(f...  19.4 us
    all_to_all x1, blocking collectives, inverse(): lax.all_to_all(along_columns, 'space', split_axis=1, concat_axis=2, tiled...  18.7 us
    dot_general x1, other arithmetic, forward(): jnp.einsum('ij,bjk->bik', kernel, columns, precision=lax.Precision.HIGHEST)  17.5 us
  transfers between devices with their start and end apart: 10, of which 10 were waited for; matrix products, arithmetic and copies ran while one was open for 4% of the time, Pallas kernels for 0%

commit v1 on v0

v1 whole, which is shorter than its diff:
```python
import functools

import jax
import jax.numpy as jnp
import numpy as np
from jax import lax
from jax.experimental import pallas as pl
from jax.experimental.pallas import tpu as pltpu
from jax.sharding import PartitionSpec as P

M = 16
MESH = pl.DeviceIdType.MESH

decay_rate = 0.0005
spread_rate = 0.01


def mode_order(length):
    return np.concatenate([np.arange(0, length, 2), np.arange(1, length, 2)])


def half_kernels(length):
    half = length // 2
    product = mode_order(length)[:, None] * np.arange(half)[None, :] % length
    angles = 2.0 * np.pi / length * product
    full = (np.cos(angles) + np.sin(angles)).astype(np.float32).reshape(2, half, half)
    high = full.astype(jnp.bfloat16)
    low = (full - high.astype(np.float32)).astype(jnp.bfloat16)
    return np.stack([high, low])


def split(value):
    high = value.astype(jnp.bfloat16)
    low = (value - high.astype(jnp.float32)).astype(jnp.bfloat16)
    return high, low


def dot(a, b, transposed):
    dims = (((1,), (1 if transposed else 0,)), ((), ()))
    return lax.dot_general(a, b, dims, preferred_element_type=jnp.float32)


def dot3(a_high, a_low, b_high, b_low, transposed=False):
    return (
        dot(a_high, b_high, transposed)
        + (dot(a_low, b_high, transposed) + dot(a_high, b_low, transposed))
    )


def mgrit_kernel(
    turns, shards,
    guess, start, source, kernels_hbm, rows_hbm, columns_ref, out_ref,
    field, kernels, row_sines, sums_high, sums_low, along, gathered, spectra, states, spread, returned,
    load_sem, kernel_sem, rows_sem, send_one, recv_one, send_two, recv_two, own_sem,
):
    tm, space = lax.axis_index("tm"), lax.axis_index("space")
    devices = turns * shards
    me = tm * shards + space
    group = devices // 2
    my_half = me // group
    rows, length = field.shape
    half = length // 2
    width = length // devices

    kernel_load = pltpu.make_async_copy(kernels_hbm, kernels, kernel_sem)
    kernel_load.start()
    rows_load = pltpu.make_async_copy(
        rows_hbm.at[pl.ds(pl.multiple_of(me * width, width), width), :], row_sines, rows_sem)
    rows_load.start()

    barrier = pltpu.get_barrier_semaphore()

    def greet(step, carry):
        peer = lax.rem(me + step, devices)
        pl.semaphore_signal(barrier, inc=1, device_id=(peer // shards, lax.rem(peer, shards)), device_id_type=MESH)
        return carry

    lax.fori_loop(1, devices, greet, 0)

    @pl.when(tm < turns - 2)
    def _():
        load = pltpu.make_async_copy(guess.at[0], field, load_sem)
        load.start()
        load.wait()

    @pl.when(tm == turns - 2)
    def _():
        load = pltpu.make_async_copy(start, field, load_sem)
        load.start()
        load.wait()

    @pl.when(tm == turns - 1)
    def _():
        load = pltpu.make_async_copy(source, field, load_sem)
        load.start()
        load.wait()

    first, second = field[:, :half], field[:, half:]
    sums_high[0, :rows], sums_low[0, :rows] = split(first + second)
    sums_high[1, :rows], sums_low[1, :rows] = split(first - second)
    kernel_load.wait()

    def first_copy(peer):
        return pltpu.make_async_remote_copy(
            src_ref=along.at[pl.ds(pl.multiple_of(peer * width, width), width), :],
            dst_ref=gathered.at[space, pl.ds(pl.multiple_of(tm * width, width), width), :],
            send_sem=send_one.at[peer], recv_sem=recv_one.at[me],
            device_id=(peer // shards, lax.rem(peer, shards)), device_id_type=MESH)

    def second_copy(peer):
        turn, shard = peer // shards, lax.rem(peer, shards)
        return pltpu.make_async_remote_copy(
            src_ref=spread.at[shard, pl.ds(pl.multiple_of(turn * width, width), width), :],
            dst_ref=returned.at[pl.ds(pl.multiple_of(me * width, width), width), :],
            send_sem=send_two.at[peer], recv_sem=recv_two.at[me],
            device_id=(turn, shard), device_id_type=MESH)

    def send_half(which, copy_to):
        def send(step, carry):
            peer = which * group + lax.rem(me + step, group)

            @pl.when(peer != me)
            def _():
                copy_to(peer).start()

            return carry

        lax.fori_loop(0, group, send, 0)

    tile = min(half, 256)
    for turn in range(2):
        which = lax.rem(my_half + 1 + turn, 2)

        def row_tile(index, carry, which=which):
            offset = pl.multiple_of(index * tile, tile)
            result = dot3(
                kernels[0, which, pl.ds(offset, tile), :], kernels[1, which, pl.ds(offset, tile), :],
                sums_high[which, :rows], sums_low[which, :rows], True)
            along[pl.ds(pl.multiple_of(which * half + index * tile, tile), tile), :] = result
            return carry

        lax.fori_loop(0, half // tile, row_tile, 0)
        if turn == 0:
            pl.semaphore_wait(barrier, devices - 1)
        send_half(which, first_copy)

    own = pltpu.make_async_copy(
        along.at[pl.ds(pl.multiple_of(me * width, width), width), :],
        gathered.at[space, pl.ds(pl.multiple_of(tm * width, width), width), :], own_sem.at[0])
    own.start()
    own.wait()
    rows_load.wait()

    def arrive_one(step, carry):
        peer = lax.rem(me + step, devices)
        pltpu.make_async_remote_copy(
            src_ref=along.at[pl.ds(pl.multiple_of(me * width, width), width), :],
            dst_ref=gathered.at[lax.rem(peer, shards), pl.ds(pl.multiple_of(peer // shards * width, width), width), :],
            send_sem=send_one.at[peer], recv_sem=recv_one.at[peer],
            device_id=(peer // shards, lax.rem(peer, shards)), device_id_type=MESH).wait_recv()
        return carry

    lax.fori_loop(1, devices, arrive_one, 0)

    batch = turns * width
    for shard in range(shards // 2):
        columns = slice(shard * rows, (shard + 1) * rows)
        upper, lower = gathered[shard], gathered[shard + shards // 2]
        sums_high[0, :batch, columns], sums_low[0, :batch, columns] = split(upper + lower)
        sums_high[1, :batch, columns], sums_low[1, :batch, columns] = split(upper - lower)
    for which in range(2):
        def column_tile(index, carry, which=which):
            offset = pl.multiple_of(index * tile, tile)
            spectra[:, pl.ds(pl.multiple_of(which * half + index * tile, tile), tile)] = dot3(
                sums_high[which, :batch], sums_low[which, :batch],
                kernels[0, which, pl.ds(offset, tile), :], kernels[1, which, pl.ds(offset, tile), :], True)
            return carry

        lax.fori_loop(0, half // tile, column_tile, 0)

    lanes = 256
    scale = 1.0 / float(length * length)

    def mix(index, carry):
        row = pl.multiple_of(index // (length // lanes) * 8, 8)
        lane = pl.ds(pl.multiple_of(lax.rem(index, length // lanes) * lanes, lanes), lanes)
        row_part = jnp.concatenate([row_sines[pl.ds(row, 8), :]] * (lanes // 128), axis=1)
        stiffness = 4.0 * (columns_ref[:, lane] + row_part)
        fine_factor = 1.0 / (1.0 + decay_rate + spread_rate * stiffness)
        coarse = 1.0 / (1.0 + M * decay_rate + M * spread_rate * stiffness)
        fine = fine_factor
        symbol = fine
        for _ in range(M - 1):
            fine = fine * fine_factor
            symbol = symbol + fine

        def slot(turn):
            return pl.ds(pl.multiple_of(turn * width + row, 8), 8)

        initial = scale * spectra[slot(turns - 2), lane]
        forcing = symbol * (scale * spectra[slot(turns - 1), lane])
        state = fine * initial + forcing
        states[slot(0), lane] = state
        state = fine * state + forcing
        states[slot(1), lane] = state
        gain = (fine * scale) * (fine - coarse)
        source_gain = (1.0 + fine - coarse) * forcing
        for turn in range(2, turns):
            state = coarse * state + (gain * spectra[slot(turn - 2), lane] + source_gain)
            states[slot(turn), lane] = state
        return carry

    lax.fori_loop(0, width // 8 * (length // lanes), mix, 0)

    part = batch // 2
    for turn in range(2):
        which = lax.rem(my_half + 1 + turn, 2)
        block = pl.ds(pl.multiple_of(which * part, part), part)
        even_high, even_low = split(states[block, :half])
        odd_high, odd_low = split(states[block, half:])
        for shard in range(shards // 2):
            columns = slice(shard * rows, (shard + 1) * rows)
            even = dot3(even_high, even_low, kernels[0, 0, :, columns], kernels[1, 0, :, columns])
            odd = dot3(odd_high, odd_low, kernels[0, 1, :, columns], kernels[1, 1, :, columns])
            spread[shard, block, :] = even + odd
            spread[shard + shards // 2, block, :] = even - odd
        send_half(which, second_copy)

    own = pltpu.make_async_copy(
        spread.at[space, pl.ds(pl.multiple_of(tm * width, width), width), :],
        returned.at[pl.ds(pl.multiple_of(me * width, width), width), :], own_sem.at[1])
    own.start()
    own.wait()

    def arrive_two(step, carry):
        peer = lax.rem(me + step, devices)
        pltpu.make_async_remote_copy(
            src_ref=spread.at[0, pl.ds(0, width), :],
            dst_ref=returned.at[pl.ds(pl.multiple_of(peer * width, width), width), :],
            send_sem=send_two.at[peer], recv_sem=recv_two.at[peer],
            device_id=(peer // shards, lax.rem(peer, shards)), device_id_type=MESH).wait_recv()
        return carry

    lax.fori_loop(1, devices, arrive_two, 0)

    even_high, even_low = split(returned[:half, :].T)
    odd_high, odd_low = split(returned[half:, :].T)
    for index in range(half // tile):
        columns = slice(index * tile, (index + 1) * tile)
        even = dot3(even_high, even_low, kernels[0, 0, :, columns], kernels[1, 0, :, columns])
        odd = dot3(odd_high, odd_low, kernels[0, 1, :, columns], kernels[1, 1, :, columns])
        out_ref[0, :, index * tile:(index + 1) * tile] = even + odd
        out_ref[0, :, half + index * tile:half + (index + 1) * tile] = even - odd

    def sent(step, carry):
        peer = lax.rem(me + step, devices)
        first_copy(peer).wait_send()
        second_copy(peer).wait_send()
        return carry

    lax.fori_loop(1, devices, sent, 0)


def body(turns, shards, initial_guess, start_field, source_field):
    rows, length = start_field.shape
    devices = turns * shards
    half, width = length // 2, length // devices
    batch = turns * width
    kernels = jnp.asarray(half_kernels(length))
    sines = (np.sin(np.pi * mode_order(length) / length) ** 2).astype(np.float32)
    row_sines = jnp.asarray(np.repeat(sines[:, None], 128, axis=1))
    column_sines = jnp.asarray(np.repeat(sines[None, :], 8, axis=0))
    tall = max(rows, batch)
    dma = pltpu.SemaphoreType.DMA
    anywhere = pl.BlockSpec(memory_space=pl.ANY)
    local = pl.BlockSpec(memory_space=pltpu.VMEM)
    return pl.pallas_call(
        functools.partial(mgrit_kernel, turns, shards),
        out_shape=jax.ShapeDtypeStruct(initial_guess.shape, jnp.float32),
        in_specs=[anywhere] * 5 + [local],
        out_specs=local,
        scratch_shapes=[
            pltpu.VMEM((rows, length), jnp.float32),
            pltpu.VMEM((2, 2, half, half), jnp.bfloat16),
            pltpu.VMEM((width, 128), jnp.float32),
            pltpu.VMEM((2, tall, half), jnp.bfloat16),
            pltpu.VMEM((2, tall, half), jnp.bfloat16),
            pltpu.VMEM((length, rows), jnp.float32),
            pltpu.VMEM((shards, batch, rows), jnp.float32),
            pltpu.VMEM((batch, length), jnp.float32),
            pltpu.VMEM((batch, length), jnp.float32),
            pltpu.VMEM((shards, batch, rows), jnp.float32),
            pltpu.VMEM((length, rows), jnp.float32),
            dma, dma, dma, dma((devices,)), dma((devices,)), dma((devices,)), dma((devices,)), dma((2,)),
        ],
        compiler_params=pltpu.CompilerParams(
            collective_id=0, has_side_effects=True, vmem_limit_bytes=32 * 1024 * 1024),
    )(initial_guess, start_field, source_field, kernels, row_sines, column_sines)


def solution(mesh):
    return jax.shard_map(
        functools.partial(body, mesh.shape["tm"], mesh.shape["space"]),
        mesh=mesh,
        in_specs=(P("tm", "space", None), P("space", None), P("space", None)),
        out_specs=P("tm", "space", None),
        check_vma=False,
    )
```

time: 409 us -> 69.6 us (0.17)
  the two profiles are of different devices: /device:TPU:16 before, /device:TPU:0 now
where the time goes in v1:
time: 69.6 us; the launch traced here: 69.2 us
  Pallas kernels  61.2 us (88%)
  local copies, waits for them, and re-layouts  8.03 us (12%)
    pallas_call x1, Pallas kernels, body(): pl.pallas_call(functools.partial(mgrit_kernel, turns, shards), out_shape=...  61.2 us
    unnamed x13, local copies, waits for them, and re-layouts  8.03 us

profile of v1, /device:TPU:0, one launch (start us, length us, event | category | flops | bytes accessed | tf_op | source)
XLA Modules:
  0.0 69.2 jit_solution(1519401106062379320)
XLA Ops:
  0.0 0.0 copy-start
  0.0 1.6 %copy-done = bf16[2,2,512,512]{3,2,1,0:T(8,128)(2,1)S(1)} copy-done((bf16[2,2,512,512]{3,2,1,0:T(8,128)(2,1)S(1)}, bf16[2,2,512,512]{3,2,1,0:T(8,128)(2,1)}, u32[]{:S(2)}) %copy-start) | copy-done | bytes 2097176
  1.6 0.0 copy-start.1
  1.6 1.2 %copy-done.1 = f32[1,256,1024]{2,1,0:T(8,128)S(1)} copy-done((f32[1,256,1024]{2,1,0:T(8,128)S(1)}, f32[1,256,1024]{2,1,0:T(8,128)}, u32[]{:S(2)}) %copy-start.1) | copy-done | bytes 1048600
  2.8 0.0 copy-start.2
  2.8 1.2 %copy-done.2 = f32[256,1024]{1,0:T(8,128)S(1)} copy-done((f32[256,1024]{1,0:T(8,128)S(1)}, f32[256,1024]{1,0:T(8,128)}, u32[]{:S(2)}) %copy-start.2) | copy-done | bytes 1048600
  4.0 0.0 copy-start.3
  4.0 1.2 %copy-done.3 = f32[256,1024]{1,0:T(8,128)S(1)} copy-done((f32[256,1024]{1,0:T(8,128)S(1)}, f32[256,1024]{1,0:T(8,128)}, u32[]{:S(2)}) %copy-start.3) | copy-done | bytes 1048600
  5.3 0.0 copy-start.4
  5.3 1.0 %copy-done.4 = f32[1024,128]{1,0:T(8,128)S(1)} copy-done((f32[1024,128]{1,0:T(8,128)S(1)}, f32[1024,128]{1,0:T(8,128)}, u32[]{:S(2)}) %copy-start.4) | copy-done | bytes 524312
  6.3 0.0 copy-start.5
  6.3 0.8 %copy-done.5 = f32[8,1024]{1,0:T(8,128)S(1)} copy-done((f32[8,1024]{1,0:T(8,128)S(1)}, f32[8,1024]{1,0:T(8,128)}, u32[]{:S(2)}) %copy-start.5) | copy-done | bytes 32792
  7.1 61.2 %shard_map.64 = f32[1,256,1024]{2,1,0:T(8,128)S(1)} custom-call(f32[1,256,1024]{2,1,0:T(8,128)S(1)} %copy-done.1, f32[256,1024]{1,0:T(8,128)S(1)} %copy-done.2, f32[256,1024]{1,0:T(8,128)S(1)} %copy-done.3, bf16[2,2,512,512]{3,2,1,0:T(8,128)(2,1)S(1)} %copy-done, f32[1024,128]{1,0:T(8,128)S(1)} %copy-done.4, f32[8,1024]{1,0:T(8,128)S(1)} %copy-done.5), custom_call_target="tpu_custom_call" | custom-call | tf_op jit(solution)/shard_map/pallas_call | solution.py:277
  68.3 1.0 %copy.8 = f32[1,256,1024]{2,1,0:T(8,128)} copy(f32[1,256,1024]{2,1,0:T(8,128)S(1)} %shard_map.64) | data formatting | bytes 2097152
Async XLA Ops:
  0.0 1.6 %copy-start = (bf16[2,2,512,512]{3,2,1,0:T(8,128)(2,1)S(1)}, bf16[2,2,512,512]{3,2,1,0:T(8,128)(2,1)}, u32[]{:S(2)}) copy-start(bf16[2,2,512,512]{3,2,1,0:T(8,128)(2,1)} %constant.6.clone.kernels_hbm) | copy-start | bytes 6291460
  1.6 1.2 %copy-start.1 = (f32[1,256,1024]{2,1,0:T(8,128)S(1)}, f32[1,256,1024]{2,1,0:T(8,128)}, u32[]{:S(2)}) copy-start(f32[1,256,1024]{2,1,0:T(8,128)} %guess.1) | copy-start | bytes 3145732
  2.8 1.2 %copy-start.2 = (f32[256,1024]{1,0:T(8,128)S(1)}, f32[256,1024]{1,0:T(8,128)}, u32[]{:S(2)}) copy-start(f32[256,1024]{1,0:T(8,128)} %start.1) | copy-start | bytes 3145732
  4.0 1.2 %copy-start.3 = (f32[256,1024]{1,0:T(8,128)S(1)}, f32[256,1024]{1,0:T(8,128)}, u32[]{:S(2)}) copy-start(f32[256,1024]{1,0:T(8,128)} %source.1) | copy-start | bytes 3145732
  5.3 1.0 %copy-start.4 = (f32[1024,128]{1,0:T(8,128)S(1)}, f32[1024,128]{1,0:T(8,128)}, u32[]{:S(2)}) copy-start(f32[1024,128]{1,0:T(8,128)} %constant.7.clone.rows_hbm) | copy-start | bytes 1572868
  6.3 0.8 %copy-start.5 = (f32[8,1024]{1,0:T(8,128)S(1)}, f32[8,1024]{1,0:T(8,128)}, u32[]{:S(2)}) copy-start(f32[8,1024]{1,0:T(8,128)} %constant.8.clone.columns_ref) | copy-start | bytes 98308

commit v2 on v1

v2 whole, which is shorter than its diff:
```python
import functools

import jax
import jax.numpy as jnp
import numpy as np
from jax import lax
from jax.experimental import pallas as pl
from jax.experimental.pallas import tpu as pltpu
from jax.sharding import PartitionSpec as P

M = 16
MESH = pl.DeviceIdType.MESH

decay_rate = 0.0005
spread_rate = 0.01


def mode_order(length):
    return np.concatenate([np.arange(0, length, 2), np.arange(1, length, 2)])


def half_kernels(length):
    half = length // 2
    product = mode_order(length)[:, None] * np.arange(half)[None, :] % length
    angles = 2.0 * np.pi / length * product
    full = (np.cos(angles) + np.sin(angles)).astype(np.float32).reshape(2, half, half)
    high = full.astype(jnp.bfloat16)
    low = (full - high.astype(np.float32)).astype(jnp.bfloat16)
    return np.stack([high, low])


def split(value):
    high = value.astype(jnp.bfloat16)
    low = (value - high.astype(jnp.float32)).astype(jnp.bfloat16)
    return high, low


def dot(a, b, transposed):
    dims = (((1,), (1 if transposed else 0,)), ((), ()))
    return lax.dot_general(a, b, dims, preferred_element_type=jnp.float32)


def dot3(a_high, a_low, b_high, b_low, transposed=False):
    return (
        dot(a_high, b_high, transposed)
        + (dot(a_low, b_high, transposed) + dot(a_high, b_low, transposed))
    )


def mgrit_kernel(
    turns, shards, chunks,
    guess, start, source, kernels_hbm, rows_hbm, columns_hbm, out_ref,
    field, kernels, row_sines, column_sines, sums_high, sums_low, along, gathered, spectra, states, spread, returned,
    load_sem, kernel_sem, rows_sem, columns_sem, send_one, recv_one, send_two, recv_two, own_sem,
):
    tm, space = lax.axis_index("tm"), lax.axis_index("space")
    devices = turns * shards
    me = tm * shards + space
    group = devices // 2
    my_half = me // group
    rows, length = field.shape
    half = length // 2
    width = length // devices

    kernel_load = pltpu.make_async_copy(kernels_hbm, kernels, kernel_sem)
    kernel_load.start()
    rows_load = pltpu.make_async_copy(
        rows_hbm.at[pl.ds(pl.multiple_of(me * width, width), width), :], row_sines, rows_sem)
    rows_load.start()
    columns_load = pltpu.make_async_copy(columns_hbm, column_sines, columns_sem)
    columns_load.start()

    barrier = pltpu.get_barrier_semaphore()

    def greet(step, carry):
        peer = lax.rem(me + step, devices)
        pl.semaphore_signal(barrier, inc=1, device_id=(peer // shards, lax.rem(peer, shards)), device_id_type=MESH)
        return carry

    lax.fori_loop(1, devices, greet, 0)

    @pl.when(tm < turns - 2)
    def _():
        load = pltpu.make_async_copy(guess.at[0], field, load_sem)
        load.start()
        load.wait()

    @pl.when(tm == turns - 2)
    def _():
        load = pltpu.make_async_copy(start, field, load_sem)
        load.start()
        load.wait()

    @pl.when(tm == turns - 1)
    def _():
        load = pltpu.make_async_copy(source, field, load_sem)
        load.start()
        load.wait()

    first, second = field[:, :half], field[:, half:]
    sums_high[0, :rows], sums_low[0, :rows] = split(first + second)
    sums_high[1, :rows], sums_low[1, :rows] = split(first - second)
    kernel_load.wait()

    def first_copy(peer):
        return pltpu.make_async_remote_copy(
            src_ref=along.at[pl.ds(pl.multiple_of(peer * width, width), width), :],
            dst_ref=gathered.at[space, pl.ds(pl.multiple_of(tm * width, width), width), :],
            send_sem=send_one.at[peer], recv_sem=recv_one.at[me],
            device_id=(peer // shards, lax.rem(peer, shards)), device_id_type=MESH)

    def second_copy(peer, chunk):
        turn, shard = peer // shards, lax.rem(peer, shards)
        return pltpu.make_async_remote_copy(
            src_ref=spread.at[shard, pl.ds(pl.multiple_of(chunk * chunk_rows + turn * deep, deep), deep), :],
            dst_ref=returned.at[pl.ds(pl.multiple_of(me * width + chunk * deep, deep), deep), :],
            send_sem=send_two.at[chunk, peer], recv_sem=recv_two.at[chunk, me],
            device_id=(turn, shard), device_id_type=MESH)

    def send_range(lowest, count, copy_to):
        def send(step, carry):
            peer = lowest + lax.rem(me + step, count)

            @pl.when(peer != me)
            def _():
                copy_to(peer).start()

            return carry

        lax.fori_loop(0, count, send, 0)

    def arrive(which, copy_from):
        def wait(step, carry):
            peer = which * group + lax.rem(me + step, group)

            @pl.when(peer != me)
            def _():
                copy_from(peer).wait_recv()

            return carry

        lax.fori_loop(0, group, wait, 0)

    batch = turns * width
    part = batch // 2
    deep = width // chunks
    chunk_rows = turns * deep
    chunk_part = chunk_rows // 2
    tile = min(half, 256)
    plane = tile // width

    pl.semaphore_wait(barrier, devices - 1)
    for turn in range(2):
        which = lax.rem(my_half + 1 + turn, 2)

        def row_tile(index, carry, which=which):
            offset = pl.multiple_of(index * tile, tile)
            result = dot3(
                kernels[0, which, pl.ds(offset, tile), :], kernels[1, which, pl.ds(offset, tile), :],
                sums_high[which, :rows], sums_low[which, :rows], True)
            along[pl.ds(pl.multiple_of(which * half + index * tile, tile), tile), :] = result
            send_range(which * group + index * plane, plane, first_copy)
            return carry

        lax.fori_loop(0, half // tile, row_tile, 0)

    own = pltpu.make_async_copy(
        along.at[pl.ds(pl.multiple_of(me * width, width), width), :],
        gathered.at[space, pl.ds(pl.multiple_of(tm * width, width), width), :], own_sem.at[0])
    own.start()
    own.wait()
    rows_load.wait()
    columns_load.wait()

    def first_from(peer):
        return pltpu.make_async_remote_copy(
            src_ref=along.at[pl.ds(pl.multiple_of(me * width, width), width), :],
            dst_ref=gathered.at[lax.rem(peer, shards), pl.ds(pl.multiple_of(peer // shards * width, width), width), :],
            send_sem=send_one.at[peer], recv_sem=recv_one.at[peer],
            device_id=(peer // shards, lax.rem(peer, shards)), device_id_type=MESH)

    for turn in range(2):
        side = lax.rem(my_half + turn, 2)
        arrive(side, first_from)
        block = pl.ds(pl.multiple_of(side * part, part), part)
        for shard in range(shards // 2):
            columns = slice(shard * rows, (shard + 1) * rows)
            upper, lower = gathered[shard, block, :], gathered[shard + shards // 2, block, :]
            sums_high[0, :part, columns], sums_low[0, :part, columns] = split(upper + lower)
            sums_high[1, :part, columns], sums_low[1, :part, columns] = split(upper - lower)
        for which in range(2):
            def column_tile(index, carry, which=which, block=block):
                offset = pl.multiple_of(index * tile, tile)
                spectra[block, pl.ds(pl.multiple_of(which * half + index * tile, tile), tile)] = dot3(
                    sums_high[which, :part], sums_low[which, :part],
                    kernels[0, which, pl.ds(offset, tile), :], kernels[1, which, pl.ds(offset, tile), :], True)
                return carry

            lax.fori_loop(0, half // tile, column_tile, 0)

    lanes = 256
    scale = 1.0 / float(length * length)

    def mix(chunk, index, carry):
        row = pl.multiple_of(index // (length // lanes) * 8, 8)
        lane = pl.ds(pl.multiple_of(lax.rem(index, length // lanes) * lanes, lanes), lanes)
        row_part = jnp.concatenate([row_sines[pl.ds(chunk * deep + row, 8), :]] * (lanes // 128), axis=1)
        stiffness = 4.0 * (column_sines[:, lane] + row_part)
        fine_factor = 1.0 / (1.0 + decay_rate + spread_rate * stiffness)
        coarse = 1.0 / (1.0 + M * decay_rate + M * spread_rate * stiffness)
        fine = fine_factor
        symbol = fine
        for _ in range(M - 1):
            fine = fine * fine_factor
            symbol = symbol + fine

        def read(turn):
            return spectra[pl.ds(pl.multiple_of(turn * width + chunk * deep + row, 8), 8), lane]

        def write(turn, value):
            states[pl.ds(pl.multiple_of(chunk * chunk_rows + turn * deep + row, 8), 8), lane] = value

        initial = scale * read(turns - 2)
        forcing = symbol * (scale * read(turns - 1))
        state = fine * initial + forcing
        write(0, state)
        state = fine * state + forcing
        write(1, state)
        gain = (fine * scale) * (fine - coarse)
        source_gain = (1.0 + fine - coarse) * forcing
        for turn in range(2, turns):
            state = coarse * state + (gain * read(turn - 2) + source_gain)
            write(turn, state)
        return carry

    def undo_columns(chunk, which):
        block = pl.ds(pl.multiple_of(chunk * chunk_rows + which * chunk_part, chunk_part), chunk_part)
        even_high, even_low = split(states[block, :half])
        odd_high, odd_low = split(states[block, half:])
        for shard in range(shards // 2):
            columns = slice(shard * rows, (shard + 1) * rows)
            even = dot3(even_high, even_low, kernels[0, 0, :, columns], kernels[1, 0, :, columns])
            odd = dot3(odd_high, odd_low, kernels[0, 1, :, columns], kernels[1, 1, :, columns])
            spread[shard, block, :] = even + odd
            spread[shard + shards // 2, block, :] = even - odd
        send_range(which * group, group, functools.partial(second_copy, chunk=chunk))

    for chunk in range(chunks):
        lax.fori_loop(0, deep // 8 * (length // lanes), functools.partial(mix, chunk), 0)
        undo_columns(chunk, 1 - my_half)
    for chunk in range(chunks):
        undo_columns(chunk, my_half)

    for chunk in range(chunks):
        own = pltpu.make_async_copy(
            spread.at[space, pl.ds(pl.multiple_of(chunk * chunk_rows + tm * deep, deep), deep), :],
            returned.at[pl.ds(pl.multiple_of(me * width + chunk * deep, deep), deep), :], own_sem.at[1 + chunk])
        own.start()
        own.wait()

    def second_from(peer, chunk):
        return pltpu.make_async_remote_copy(
            src_ref=spread.at[0, pl.ds(0, deep), :],
            dst_ref=returned.at[pl.ds(pl.multiple_of(peer * width + chunk * deep, deep), deep), :],
            send_sem=send_two.at[chunk, peer], recv_sem=recv_two.at[chunk, peer],
            device_id=(peer // shards, lax.rem(peer, shards)), device_id_type=MESH)

    def undo_rows(which):
        for chunk in range(chunks):
            arrive(which, functools.partial(second_from, chunk=chunk))
        high, low = split(returned[pl.ds(pl.multiple_of(which * half, half), half), :].T)
        return [
            dot3(high, low, kernels[0, which, :, columns], kernels[1, which, :, columns])
            for columns in (slice(index, index + tile) for index in range(0, half, tile))
        ]

    for index, near in enumerate(undo_rows(my_half)):
        field[:, index * tile:(index + 1) * tile] = near
    sign = 1.0 - 2.0 * my_half.astype(jnp.float32)
    for index, far in enumerate(undo_rows(1 - my_half)):
        near = field[:, index * tile:(index + 1) * tile]
        out_ref[0, :, index * tile:(index + 1) * tile] = near + far
        out_ref[0, :, half + index * tile:half + (index + 1) * tile] = sign * (near - far)

    def sent(step, carry):
        peer = lax.rem(me + step, devices)
        first_copy(peer).wait_send()
        for chunk in range(chunks):
            second_copy(peer, chunk).wait_send()
        return carry

    lax.fori_loop(1, devices, sent, 0)


def body(turns, shards, initial_guess, start_field, source_field):
    rows, length = start_field.shape
    devices = turns * shards
    half, width = length // 2, length // devices
    batch = turns * width
    kernels = jnp.asarray(half_kernels(length))
    sines = (np.sin(np.pi * mode_order(length) / length) ** 2).astype(np.float32)
    row_sines = jnp.asarray(np.repeat(sines[:, None], 128, axis=1))
    column_sines = jnp.asarray(np.repeat(sines[None, :], 8, axis=0))
    chunks = 2 if width % 16 == 0 else 1
    tall = max(rows, batch)
    dma = pltpu.SemaphoreType.DMA
    anywhere = pl.BlockSpec(memory_space=pltpu.HBM)
    local = pl.BlockSpec(memory_space=pltpu.VMEM)
    return pl.pallas_call(
        functools.partial(mgrit_kernel, turns, shards, chunks),
        out_shape=jax.ShapeDtypeStruct(initial_guess.shape, jnp.float32),
        in_specs=[anywhere] * 6,
        out_specs=local,
        scratch_shapes=[
            pltpu.VMEM((rows, length), jnp.float32),
            pltpu.VMEM((2, 2, half, half), jnp.bfloat16),
            pltpu.VMEM((width, 128), jnp.float32),
            pltpu.VMEM((8, length), jnp.float32),
            pltpu.VMEM((2, tall, half), jnp.bfloat16),
            pltpu.VMEM((2, tall, half), jnp.bfloat16),
            pltpu.VMEM((length, rows), jnp.float32),
            pltpu.VMEM((shards, batch, rows), jnp.float32),
            pltpu.VMEM((batch, length), jnp.float32),
            pltpu.VMEM((batch, length), jnp.float32),
            pltpu.VMEM((shards, batch, rows), jnp.float32),
            pltpu.VMEM((length, rows), jnp.float32),
            dma, dma, dma, dma, dma((devices,)), dma((devices,)),
            dma((chunks, devices)), dma((chunks, devices)), dma((1 + chunks,)),
        ],
        compiler_params=pltpu.CompilerParams(
            collective_id=0, has_side_effects=True, vmem_limit_bytes=60 * 1024 * 1024),
    )(initial_guess, start_field, source_field, kernels, row_sines, column_sines)


def solution(mesh):
    return jax.shard_map(
        functools.partial(body, mesh.shape["tm"], mesh.shape["space"]),
        mesh=mesh,
        in_specs=(P("tm", "space", None), P("space", None), P("space", None)),
        out_specs=P("tm", "space", None),
        check_vma=False,
    )
```

time: 69.6 us -> 62.7 us (0.901)
  local copies, waits for them, and re-layouts: 8.03 us -> 2.31 us
  Pallas kernels: 61.2 us -> 60.3 us
    unnamed x13 -> x1, local copies, waits for them, and re-layouts: 8.03 us -> 2.31 us
    pallas_call x1, Pallas kernels: 61.2 us -> 60.3 us  [body(): pl.pallas_call(functools.partial(mgrit_kernel, turns, shards, chunks), ou...]
where the time goes in v2:
time: 62.7 us; the launch traced here: 62.6 us
  Pallas kernels  60.3 us (96%)
  local copies, waits for them, and re-layouts  2.31 us (4%)
    pallas_call x1, Pallas kernels, body(): pl.pallas_call(functools.partial(mgrit_kernel, turns, shards, chunks), ou...  60.3 us
    unnamed x1, local copies, waits for them, and re-layouts  2.31 us

profile of v2, /device:TPU:0, one launch (start us, length us, event | category | flops | bytes accessed | tf_op | source)
XLA Modules:
  0.0 62.6 jit_solution(2141630503441349077)
XLA Ops:
  0.0 60.3 %shard_map.64 = f32[1,256,1024]{2,1,0:T(8,128)} custom-call(f32[1,256,1024]{2,1,0:T(8,128)} %guess.1, f32[256,1024]{1,0:T(8,128)} %start.1, f32[256,1024]{1,0:T(8,128)} %source.1, bf16[2,2,512,512]{3,2,1,0:T(8,128)(2,1)} %constant.6.clone.kernels_hbm, f32[1024,128]{1,0:T(8,128)} %constant.7.clone.rows_hbm, f32[8,1024]{1,0:T(8,128)} %constant.8.clone.columns_hbm), custom_call_target="tpu_custom_call" | custom-call | tf_op jit(solution)/shard_map/pallas_call | solution.py:309
  60.3 2.3 %copy.8 = f32[1,256,1024]{2,1,0:T(8,128)} copy(f32[1,256,1024]{2,1,0:T(8,128)} %shard_map.64) | data formatting | bytes 2097152

commit v3 on v2

--- a/solution.py
+++ b/solution.py
@@ -328,8 +328,9 @@
             dma((chunks, devices)), dma((chunks, devices)), dma((1 + chunks,)),
         ],
         compiler_params=pltpu.CompilerParams(
-            collective_id=0, has_side_effects=True, vmem_limit_bytes=60 * 1024 * 1024),
-    )(initial_guess, start_field, source_field, kernels, row_sines, column_sines)
+            collective_id=0, has_side_effects=True, vmem_limit_bytes=32 * 1024 * 1024),
+    )(*(pltpu.with_memory_space_constraint(value, pltpu.HBM)
+        for value in (initial_guess, start_field, source_field, kernels, row_sines, column_sines)))
 
 
 def solution(mesh):

time: 62.7 us -> 60.4 us (0.963)
  local copies, waits for them, and re-layouts: 2.31 us -> 0.97 us
  Pallas kernels: 60.3 us -> 59.2 us
    unnamed x1, local copies, waits for them, and re-layouts: 2.31 us -> 0.97 us
    pallas_call x1, Pallas kernels: 60.3 us -> 59.2 us  [body(): pl.pallas_call(functools.partial(mgrit_kernel, turns, shards, chunks), ou...]
where the time goes in v3:
time: 60.4 us; the launch traced here: 60.2 us
  Pallas kernels  59.2 us (98%)
  local copies, waits for them, and re-layouts  0.97 us (2%)
    pallas_call x1, Pallas kernels, body(): pl.pallas_call(functools.partial(mgrit_kernel, turns, shards, chunks), ou...  59.2 us

profile of v3, /device:TPU:0, one launch (start us, length us, event | category | flops | bytes accessed | tf_op | source)
XLA Modules:
  0.0 60.2 jit_solution(7951720373528675394)
XLA Ops:
  0.0 59.2 %shard_map.64 = f32[1,256,1024]{2,1,0:T(8,128)S(1)} custom-call(f32[1,256,1024]{2,1,0:T(8,128)} %guess.1, f32[256,1024]{1,0:T(8,128)} %start.1, f32[256,1024]{1,0:T(8,128)} %source.1, bf16[2,2,512,512]{3,2,1,0:T(8,128)(2,1)} %constant.6.clone.kernels_hbm, f32[1024,128]{1,0:T(8,128)} %constant.7.clone.rows_hbm, f32[8,1024]{1,0:T(8,128)} %constant.8.clone.columns_hbm), custom_call_target="tpu_custom_call" | custom-call | tf_op jit(solution)/shard_map/pallas_call | solution.py:309
  59.2 1.0 %copy.8 = f32[1,256,1024]{2,1,0:T(8,128)} copy(f32[1,256,1024]{2,1,0:T(8,128)S(1)} %shard_map.64) | data formatting | bytes 2097152

commit v4 on v0

v4 whole, which is shorter than its diff:
```python
import functools

import jax
import jax.numpy as jnp
import numpy as np
from jax import lax
from jax.experimental import pallas as pl
from jax.experimental.pallas import tpu as pltpu
from jax.sharding import PartitionSpec as P

M = 16
MESH = pl.DeviceIdType.MESH

decay_rate = 0.0005
spread_rate = 0.01


def mode_order(length):
    return np.concatenate([np.arange(0, length, 2), np.arange(1, length, 2)])


def half_kernels(length):
    half = length // 2
    product = mode_order(length)[:, None] * np.arange(half)[None, :] % length
    angles = 2.0 * np.pi / length * product
    full = (np.cos(angles) + np.sin(angles)).astype(np.float32).reshape(2, half, half)
    high = full.astype(jnp.bfloat16)
    low = (full - high.astype(np.float32)).astype(jnp.bfloat16)
    return np.stack([high, low])


def split(value):
    high = value.astype(jnp.bfloat16)
    low = (value - high.astype(jnp.float32)).astype(jnp.bfloat16)
    return high, low


def dot(a, b, transposed):
    dims = (((1,), (1 if transposed else 0,)), ((), ()))
    return lax.dot_general(a, b, dims, preferred_element_type=jnp.float32)


def dot3(a_high, a_low, b_high, b_low, transposed=False):
    return (
        dot(a_high, b_high, transposed)
        + (dot(a_low, b_high, transposed) + dot(a_high, b_low, transposed))
    )


def mgrit_kernel(
    turns, shards, chunks,
    guess, start, source, kernels_hbm, rows_hbm, columns_hbm, out_ref,
    field, extra, kernels, row_sines, column_sines, field_high, field_low, extra_high, extra_low,
    sums_high, sums_low, along, along_extra, gathered, gathered_extra, spectra, states, crossing, incoming,
    spread, returned,
    load_sem, kernel_sem, rows_sem, columns_sem, send_one, recv_one, send_extra, recv_extra,
    send_cross, recv_cross, send_two, recv_two, own_sem,
):
    tm, space = lax.axis_index("tm"), lax.axis_index("space")
    devices = turns * shards
    group = devices // 2
    turns_here = turns // 2
    side = tm // turns_here
    place = lax.rem(tm, turns_here)
    me = place * shards + space
    rows, length = field.shape
    half = length // 2
    tile = length // chunks
    deep = tile // group
    slots = turns_here * deep
    per_parity = chunks // 2
    has_guess = tm < turns - 2

    field_load = pltpu.make_async_copy(guess.at[0], field, load_sem.at[0])
    field_load.start()
    kernel_load = pltpu.make_async_copy(kernels_hbm, kernels, kernel_sem)
    kernel_load.start()
    start_load = pltpu.make_async_copy(start, extra.at[pl.ds(0, rows), :], load_sem.at[1])
    start_load.start()
    source_load = pltpu.make_async_copy(source, extra.at[pl.ds(rows, rows), :], load_sem.at[2])
    source_load.start()
    rows_loads = []
    for chunk in range(chunks):
        load = pltpu.make_async_copy(
            rows_hbm.at[pl.ds(pl.multiple_of(chunk * tile + me * deep, deep), deep), :],
            row_sines.at[pl.ds(chunk * deep, deep), :], rows_sem.at[chunk])
        load.start()
        rows_loads.append(load)
    columns_load = pltpu.make_async_copy(columns_hbm, column_sines, columns_sem)
    columns_load.start()

    def device(peer):
        return (side * turns_here + peer // shards, lax.rem(peer, shards))

    other = (lax.rem(tm + turns_here, turns), space)
    barrier = pltpu.get_barrier_semaphore()

    def greet(step, carry):
        pl.semaphore_signal(barrier, inc=1, device_id=device(lax.rem(me + step, group)), device_id_type=MESH)
        return carry

    lax.fori_loop(1, group, greet, 0)
    pl.semaphore_signal(barrier, inc=1, device_id=other, device_id_type=MESH)

    def rows_of(base, index):
        return pl.ds(pl.multiple_of(base + index * deep, deep), deep)

    def first_copy(chunk, peer, origin=None):
        origin = me if origin is None else origin
        return pltpu.make_async_remote_copy(
            src_ref=along.at[rows_of(chunk * tile, peer), :],
            dst_ref=gathered.at[chunk, lax.rem(origin, shards), rows_of(0, origin // shards), :],
            send_sem=send_one.at[chunk, peer], recv_sem=recv_one.at[chunk, origin],
            device_id=device(peer), device_id_type=MESH)

    def extra_copy(chunk, shard, origin=None):
        origin = space if origin is None else origin
        return pltpu.make_async_remote_copy(
            src_ref=along_extra.at[chunk, rows_of(0, shard), :],
            dst_ref=gathered_extra.at[chunk, origin],
            send_sem=send_extra.at[chunk, shard], recv_sem=recv_extra.at[chunk, origin],
            device_id=(tm, shard), device_id_type=MESH)

    def cross_copy(chunk):
        return pltpu.make_async_remote_copy(
            src_ref=crossing.at[chunk], dst_ref=incoming.at[chunk],
            send_sem=send_cross.at[chunk], recv_sem=recv_cross.at[chunk],
            device_id=other, device_id_type=MESH)

    def second_copy(chunk, peer, origin=None):
        origin = me if origin is None else origin
        return pltpu.make_async_remote_copy(
            src_ref=spread.at[chunk, lax.rem(peer, shards), rows_of(0, peer // shards), :],
            dst_ref=returned.at[rows_of(chunk * tile, origin), :],
            send_sem=send_two.at[chunk, peer], recv_sem=recv_two.at[chunk, origin],
            device_id=device(peer), device_id_type=MESH)

    def around(mine, count, act):
        def turn(step, carry):
            act(lax.rem(mine + step, count))
            return carry

        lax.fori_loop(1, count, turn, 0)

    field_load.wait()
    first, second = field[:, :half], field[:, half:]
    field_high[0], field_low[0] = split(first + second)
    field_high[1], field_low[1] = split(first - second)
    kernel_load.wait()
    start_load.wait()
    source_load.wait()
    first, second = extra[:, :half], extra[:, half:]
    extra_high[0], extra_low[0] = split(first + second)
    extra_high[1], extra_low[1] = split(first - second)

    for chunk in range(chunks):
        which, offset = chunk // per_parity, chunk % per_parity * tile
        along[chunk * tile:(chunk + 1) * tile, :] = dot3(
            kernels[0, which, offset:offset + tile, :], kernels[1, which, offset:offset + tile, :],
            field_high[which], field_low[which], True)
        if chunk == 0:
            pl.semaphore_wait(barrier, group)

        @pl.when(has_guess)
        def _():
            around(me, group, lambda peer: first_copy(chunk, peer).start())

        mine = pl.ds(pl.multiple_of(offset + place * (shards * deep), shards * deep), shards * deep)
        along_extra[chunk] = dot3(
            kernels[0, which, mine, :], kernels[1, which, mine, :], extra_high[which], extra_low[which], True)
        around(space, shards, lambda shard: extra_copy(chunk, shard).start())

    for load in rows_loads:
        load.wait()
    columns_load.wait()
    owns = []
    for chunk in range(chunks):
        owns.append(pltpu.make_async_copy(
            along.at[rows_of(chunk * tile, me), :], gathered.at[chunk, space, rows_of(0, place), :],
            own_sem.at[0, chunk]))
        owns.append(pltpu.make_async_copy(
            along_extra.at[chunk, rows_of(0, space), :], gathered_extra.at[chunk, space], own_sem.at[1, chunk]))
    for own in owns:
        own.start()
    for own in owns:
        own.wait()

    lanes = 256
    across = length // lanes
    scale = 1.0 / float(length * length)

    def mix(chunk, first_side, index, carry):
        row = pl.multiple_of(index // across * 8, 8)
        lane = pl.ds(pl.multiple_of(lax.rem(index, across) * lanes, lanes), lanes)
        row_part = jnp.concatenate([row_sines[pl.ds(chunk * deep + row, 8), :]] * (lanes // 128), axis=1)
        stiffness = 4.0 * (column_sines[:, lane] + row_part)
        fine_factor = 1.0 / (1.0 + decay_rate + spread_rate * stiffness)
        coarse = 1.0 / (1.0 + M * decay_rate + M * spread_rate * stiffness)
        fine = fine_factor
        symbol = fine
        for _ in range(M - 1):
            fine = fine * fine_factor
            symbol = symbol + fine

        def at(turn):
            return pl.ds(pl.multiple_of(turn * deep + row, 8), 8)

        forcing = symbol * (scale * spectra[chunk, at(turns_here + 1), lane])
        gain = (fine * scale) * (fine - coarse)
        source_gain = (1.0 + fine - coarse) * forcing
        if first_side:
            before = fine * (scale * spectra[chunk, at(turns_here), lane]) + forcing
            state = fine * before + forcing
        else:
            before, state = incoming[chunk, at(0), lane], incoming[chunk, at(1), lane]
        states[chunk, at(0), lane] = before
        states[chunk, at(1), lane] = state
        for turn in range(2, turns_here + 2 if first_side else turns_here):
            state = coarse * state + (gain * spectra[chunk, at(turn - 2), lane] + source_gain)
            if turn < turns_here:
                states[chunk, at(turn), lane] = state
            else:
                crossing[chunk, at(turn - turns_here), lane] = state
        return carry

    steps = deep // 8 * across
    for chunk in range(chunks):
        def from_peer(peer):
            @pl.when(side * turns_here + peer // shards < turns - 2)
            def _():
                first_copy(chunk, me, peer).wait_recv()

        around(me, group, from_peer)
        around(space, shards, lambda shard: extra_copy(chunk, space, shard).wait_recv())
        for shard in range(shards // 2):
            columns = slice(shard * rows, (shard + 1) * rows)
            upper, lower = [
                jnp.concatenate(
                    [gathered[chunk, part], gathered_extra[chunk, part, :, :rows], gathered_extra[chunk, part, :, rows:]],
                    axis=0)
                for part in (shard, shard + shards // 2)
            ]
            sums_high[0, :, columns], sums_low[0, :, columns] = split(upper + lower)
            sums_high[1, :, columns], sums_low[1, :, columns] = split(upper - lower)
        for which in range(2):
            spectra[chunk, :, which * half:(which + 1) * half] = dot3(
                sums_high[which], sums_low[which], kernels[0, which], kernels[1, which], True)

        @pl.when(side == 0)
        def _():
            lax.fori_loop(0, steps, functools.partial(mix, chunk, True), 0)
            cross_copy(chunk).start()

    for chunk in range(chunks):
        @pl.when(side == 1)
        def _():
            cross_copy(chunk).wait_recv()
            lax.fori_loop(0, steps, functools.partial(mix, chunk, False), 0)

        even_high, even_low = split(states[chunk, :, :half])
        odd_high, odd_low = split(states[chunk, :, half:])
        for shard in range(shards // 2):
            columns = slice(shard * rows, (shard + 1) * rows)
            even = dot3(even_high, even_low, kernels[0, 0, :, columns], kernels[1, 0, :, columns])
            odd = dot3(odd_high, odd_low, kernels[0, 1, :, columns], kernels[1, 1, :, columns])
            spread[chunk, shard] = even + odd
            spread[chunk, shard + shards // 2] = even - odd
        around(me, group, lambda peer: second_copy(chunk, peer).start())
        own = pltpu.make_async_copy(
            spread.at[chunk, space, rows_of(0, place), :], returned.at[rows_of(chunk * tile, me), :],
            own_sem.at[2, chunk])
        own.start()
        own.wait()

    for chunk in range(chunks):
        around(me, group, lambda peer: second_copy(chunk, me, peer).wait_recv())
        which, offset = chunk // per_parity, chunk % per_parity * tile
        high, low = split(returned[chunk * tile:(chunk + 1) * tile, :].T)
        for index in range(0, half, 256):
            columns = slice(index, index + 256)
            opposite = slice(half + index, half + index + 256)
            value = dot3(
                high, low, kernels[0, which, offset:offset + tile, columns],
                kernels[1, which, offset:offset + tile, columns])
            if chunk == 0:
                field[:, columns] = value
            elif chunk < per_parity:
                field[:, columns] += value
            elif chunk < chunks - 1:
                if chunk == per_parity:
                    field[:, opposite] = value
                else:
                    field[:, opposite] += value
            else:
                odd = value if per_parity == 1 else field[:, opposite] + value
                even = field[:, columns]
                out_ref[0, :, columns] = even + odd
                out_ref[0, :, opposite] = even - odd

    for chunk in range(chunks):
        @pl.when(has_guess)
        def _():
            around(me, group, lambda peer: first_copy(chunk, peer).wait_send())

        around(space, shards, lambda shard: extra_copy(chunk, shard).wait_send())

        @pl.when(side == 0)
        def _():
            cross_copy(chunk).wait_send()

        around(me, group, lambda peer: second_copy(chunk, peer).wait_send())


def body(turns, shards, initial_guess, start_field, source_field):
    rows, length = start_field.shape
    group = turns * shards // 2
    half = length // 2
    chunks = min(4, length // group // 8)
    tile = length // chunks
    deep = tile // group
    slots = turns // 2 * deep
    kernels = jnp.asarray(half_kernels(length))
    sines = (np.sin(np.pi * mode_order(length) / length) ** 2).astype(np.float32)
    row_sines = jnp.asarray(np.repeat(sines[:, None], 128, axis=1))
    column_sines = jnp.asarray(np.repeat(sines[None, :], 8, axis=0))
    f32, bf16 = jnp.float32, jnp.bfloat16
    dma = pltpu.SemaphoreType.DMA
    return pl.pallas_call(
        functools.partial(mgrit_kernel, turns, shards, chunks),
        out_shape=jax.ShapeDtypeStruct(initial_guess.shape, f32),
        in_specs=[pl.BlockSpec(memory_space=pltpu.HBM)] * 6,
        out_specs=pl.BlockSpec(memory_space=pltpu.VMEM),
        scratch_shapes=[
            pltpu.VMEM((rows, length), f32),
            pltpu.VMEM((2 * rows, length), f32),
            pltpu.VMEM((2, 2, half, half), bf16),
            pltpu.VMEM((chunks * deep, 128), f32),
            pltpu.VMEM((8, length), f32),
            pltpu.VMEM((2, rows, half), bf16),
            pltpu.VMEM((2, rows, half), bf16),
            pltpu.VMEM((2, 2 * rows, half), bf16),
            pltpu.VMEM((2, 2 * rows, half), bf16),
            pltpu.VMEM((2, slots + 2 * deep, half), bf16),
            pltpu.VMEM((2, slots + 2 * deep, half), bf16),
            pltpu.VMEM((length, rows), f32),
            pltpu.VMEM((chunks, shards * deep, 2 * rows), f32),
            pltpu.VMEM((chunks, shards, slots, rows), f32),
            pltpu.VMEM((chunks, shards, deep, 2 * rows), f32),
            pltpu.VMEM((chunks, slots + 2 * deep, length), f32),
            pltpu.VMEM((chunks, slots, length), f32),
            pltpu.VMEM((chunks, 2 * deep, length), f32),
            pltpu.VMEM((chunks, 2 * deep, length), f32),
            pltpu.VMEM((chunks, shards, slots, rows), f32),
            pltpu.VMEM((length, rows), f32),
            dma((3,)), dma, dma((chunks,)), dma, dma((chunks, group)), dma((chunks, group)),
            dma((chunks, shards)), dma((chunks, shards)), dma((chunks,)), dma((chunks,)),
            dma((chunks, group)), dma((chunks, group)), dma((3, chunks)),
        ],
        compiler_params=pltpu.CompilerParams(
            collective_id=0, has_side_effects=True, vmem_limit_bytes=40 * 1024 * 1024),
    )(*(pltpu.with_memory_space_constraint(value, pltpu.HBM)
        for value in (initial_guess, start_field, source_field, kernels, row_sines, column_sines)))


def solution(mesh):
    return jax.shard_map(
        functools.partial(body, mesh.shape["tm"], mesh.shape["space"]),
        mesh=mesh,
        in_specs=(P("tm", "space", None), P("space", None), P("space", None)),
        out_specs=P("tm", "space", None),
        check_vma=False,
    )
```

time: 409 us -> 49.7 us (0.12)
  the two profiles are of different devices: /device:TPU:16 before, /device:TPU:21 now
where the time goes in v4:
time: 49.7 us; the launch traced here: 49.5 us
  Pallas kernels  48.6 us (98%)
  local copies, waits for them, and re-layouts  0.97 us (2%)
    pallas_call x1, Pallas kernels, body(): pl.pallas_call(functools.partial(mgrit_kernel, turns, shards, chunks), ou...  48.6 us

profile of v4, /device:TPU:21, one launch (start us, length us, event | category | flops | bytes accessed | tf_op | source)
XLA Modules:
  0.0 49.5 jit_solution(6625773950948850781)
XLA Ops:
  0.0 48.6 %shard_map.64 = f32[1,256,1024]{2,1,0:T(8,128)S(1)} custom-call(f32[1,256,1024]{2,1,0:T(8,128)} %guess.1, f32[256,1024]{1,0:T(8,128)} %start.1, f32[256,1024]{1,0:T(8,128)} %source.1, bf16[2,2,512,512]{3,2,1,0:T(8,128)(2,1)} %constant.6.clone.kernels_hbm, f32[1024,128]{1,0:T(8,128)} %constant.7.clone.rows_hbm, f32[8,1024]{1,0:T(8,128)} %constant.8.clone.columns_hbm), custom_call_target="tpu_custom_call" | custom-call | tf_op jit(solution)/shard_map/pallas_call | solution.py:328
  48.6 1.0 %copy.8 = f32[1,256,1024]{2,1,0:T(8,128)} copy(f32[1,256,1024]{2,1,0:T(8,128)S(1)} %shard_map.64) | data formatting | bytes 2097152

commit v5 on v4

--- a/solution.py
+++ b/solution.py
@@ -147,11 +147,6 @@
     field_high[0], field_low[0] = split(first + second)
     field_high[1], field_low[1] = split(first - second)
     kernel_load.wait()
-    start_load.wait()
-    source_load.wait()
-    first, second = extra[:, :half], extra[:, half:]
-    extra_high[0], extra_low[0] = split(first + second)
-    extra_high[1], extra_low[1] = split(first - second)
 
     for chunk in range(chunks):
         which, offset = chunk // per_parity, chunk % per_parity * tile
@@ -165,6 +160,12 @@
         def _():
             around(me, group, lambda peer: first_copy(chunk, peer).start())
 
+        if chunk == 0:
+            start_load.wait()
+            source_load.wait()
+            first, second = extra[:, :half], extra[:, half:]
+            extra_high[0], extra_low[0] = split(first + second)
+            extra_high[1], extra_low[1] = split(first - second)
         mine = pl.ds(pl.multiple_of(offset + place * (shards * deep), shards * deep), shards * deep)
         along_extra[chunk] = dot3(
             kernels[0, which, mine, :], kernels[1, which, mine, :], extra_high[which], extra_low[which], True)

time: 49.7 us -> 48.9 us (0.984)
  Pallas kernels: 48.6 us -> 47.8 us
    pallas_call x1, Pallas kernels: 48.6 us -> 47.8 us  [body(): pl.pallas_call(functools.partial(mgrit_kernel, turns, shards, chunks), ou...]
where the time goes in v5:
time: 48.9 us; the launch traced here: 48.8 us
  Pallas kernels  47.8 us (98%)
  local copies, waits for them, and re-layouts  0.97 us (2%)
    pallas_call x1, Pallas kernels, body(): pl.pallas_call(functools.partial(mgrit_kernel, turns, shards, chunks), ou...  47.8 us

profile of v5, /device:TPU:21, one launch (start us, length us, event | category | flops | bytes accessed | tf_op | source)
XLA Modules:
  0.0 48.8 jit_solution(16539297732117565326)
XLA Ops:
  0.0 47.8 %shard_map.64 = f32[1,256,1024]{2,1,0:T(8,128)S(1)} custom-call(f32[1,256,1024]{2,1,0:T(8,128)} %guess.1, f32[256,1024]{1,0:T(8,128)} %start.1, f32[256,1024]{1,0:T(8,128)} %source.1, bf16[2,2,512,512]{3,2,1,0:T(8,128)(2,1)} %constant.6.clone.kernels_hbm, f32[1024,128]{1,0:T(8,128)} %constant.7.clone.rows_hbm, f32[8,1024]{1,0:T(8,128)} %constant.8.clone.columns_hbm), custom_call_target="tpu_custom_call" | custom-call | tf_op jit(solution)/shard_map/pallas_call | solution.py:329
  47.8 1.0 %copy.8 = f32[1,256,1024]{2,1,0:T(8,128)} copy(f32[1,256,1024]{2,1,0:T(8,128)S(1)} %shard_map.64) | data formatting | bytes 2097152
